TPU v7x, 32 devices: a whole 2x2x4 slice. The times are simulated.
32 devices in a mesh: tile: 8 (over z, y), grp: 4 (over x, core).
Axes of the slice: x: 2, y: 2, z: 4, core: 2. Of those that a mesh axis runs over, the one named last changes fastest.
Arguments:
- left_triples: bfloat16 [256, 6144, 300], P('tile', 'grp'), may hold values from -6 to 6
- right_triples: bfloat16 [256, 6144, 300], P('tile', 'grp'), may hold values from -6 to 6
- live_tiles: int32 [256, 24], P('tile', 'grp'), may hold values from 0 to 1
- vv_block: bfloat16 [300, 300], replicated, may hold values from -0.375 to 0.375
- slab_block: bfloat16 [256, 256], replicated, may hold values from -0.375 to 0.375
- left_doubles: bfloat16 [256, 8192], P('tile', 'grp'), may hold values from -6 to 6
- ov_block: bfloat16 [30, 300], replicated, may hold values from -6 to 6
- pair_index: int32 [6144], P('grp'), may hold values from 0 to 8191
- occ_index: int32 [6144], P('grp'), may hold values from 0 to 29
Outputs:
- sigma_out: bfloat16 [256, 6144, 300], P('tile', 'grp')
- density: float32 [300, 300], replicated
All inputs are finite; a program needn't handle non-finite values.
Results may differ from a plain program's by a relative error of at most 0.0026.
Values may be sent and summed in bfloat16 or wider, within the bound.
No kernel may reach another device: no remote copies, remote signals or barrier semaphores. Data moves between devices by JAX's collectives and lax.ppermute only.
A program may use at most 320 MiB of HBM per device.

v0:
```python
import math
import jax
import jax.numpy as jnp
from jax import lax
from jax.sharding import PartitionSpec as P


def body(
    left_triples,
    right_triples,
    live_tiles,
    vv_block,
    slab_block,
    left_doubles,
    ov_block,
    pair_index,
    occ_index,
):
    slab_count, row_count, feature = left_triples.shape
    tile_count = live_tiles.shape[1]
    tile_rows = row_count // tile_count
    live_mask = live_tiles.astype(jnp.bfloat16)
    masked = (
        left_triples.reshape(slab_count, tile_count, tile_rows, feature)
        * live_mask[:, :, None, None]
    ).reshape(slab_count, row_count, feature)
    mixed_rows = jnp.einsum(
        "bd,drc->brc",
        slab_block,
        lax.all_to_all(masked, "tile", split_axis=1, concat_axis=0, tiled=True),
        preferred_element_type=jnp.float32,
    ).astype(jnp.bfloat16)
    slab_term = lax.all_to_all(mixed_rows, "tile", split_axis=0, concat_axis=1, tiled=True)
    full_table = lax.all_gather(left_doubles, "grp", axis=1, tiled=True)
    picked = jnp.take(full_table, pair_index, axis=1).astype(jnp.float32)
    onehot = (occ_index[:, None] == jnp.arange(ov_block.shape[0], dtype=jnp.int32)[None, :]).astype(
        jnp.bfloat16
    )
    occ_rows = jnp.dot(onehot, ov_block, preferred_element_type=jnp.float32)
    pair_term = picked[:, :, None] * occ_rows[None, :, :]
    flat_rows = masked.reshape(-1, feature)
    vv_term = jnp.dot(flat_rows, vv_block, preferred_element_type=jnp.float32).reshape(
        slab_count, row_count, feature
    )
    partial_value = lax.dot_general(
        flat_rows,
        right_triples.reshape(-1, feature),
        (((0,), (0,)), ((), ())),
        preferred_element_type=jnp.float32,
    )
    summed = vv_term + slab_term.astype(jnp.float32) + pair_term
    summed = (
        summed.reshape(slab_count, tile_count, tile_rows, feature)
        * live_tiles.astype(jnp.float32)[:, :, None, None]
    )
    sigma_out = summed.reshape(slab_count, row_count, feature).astype(jnp.bfloat16)
    norm_scale = math.sqrt(slab_count * lax.axis_size("tile") * row_count * lax.axis_size("grp"))
    density = lax.psum(partial_value, ("tile", "grp")) / norm_scale
    return (sigma_out, density)


def solution(mesh):
    in_specs = (
        P("tile", "grp", None),
        P("tile", "grp", None),
        P("tile", "grp"),
        P(),
        P(),
        P("tile", "grp"),
        P(),
        P("grp"),
        P("grp"),
    )
    out_specs = (P("tile", "grp", None), P())
    return jax.shard_map(body, mesh=mesh, in_specs=in_specs, out_specs=out_specs, check_vma=False)
```

profile of v0, /device:TPU:0, one launch (start us, length us, event | category | flops | bytes accessed | tf_op | source)
XLA Modules:
  0.0 2170.5 jit_solution(17723983579102497324)
XLA Ops:
  7.2 1.4 fusion.17
  8.5 0.1 copy.70
  8.6 0.1 mul.42
  8.8 20.2 broadcast_multiply_fusion
  28.9 48.6 %copy.73 = bf16[32,1536,300]{2,0,1:T(8,128)(2,1)} copy(bf16[32,1536,300]{1,0,2:T(8,128)(2,1)} %broadcast_multiply_fusion) | data formatting | bytes 58982400 | tf_op jit(solution)/shard_map/mul | solution.py:24
  77.6 825.9 %all_to_all.27 = bf16[32,1536,300]{2,0,1:T(8,128)(2,1)} all-to-all(bf16[32,1536,300]{2,0,1:T(8,128)(2,1)} %copy.73), channel_id=1, replica_groups=mesh['tile'=8,'grp'=4] {'tile'}, dimensions={1} | all-to-all | bytes 58982400 | tf_op jit(solution)/shard_map/all_to_all | solution.py:30
  903.5 25.6 %copy.75 = bf16[8,32,192,300]{3,2,1,0:T(8,128)(2,1)} copy(bf16[8,32,192,300]{3,1,2,0:T(8,128)(2,1)} %bitcast.31) | data formatting | bytes 58982400 | tf_op jit(solution)/shard_map/all_to_all | solution.py:30
  929.1 38.3 %convert_bitcast_fusion.1 = bf16[256,192,300]{0,2,1:T(8,128)(2,1)} fusion(bf16[256,192,300]{2,1,0:T(8,128)(2,1)} %bitcast.30, bf16[256,256]{1,0:T(8,128)(2,1)S(1)} %copy-done.1), kind=kOutput, calls=%fused_computation.7 | convolution fusion | flops 7564492800 | bytes 59113472 | tf_op jit(solution)/shard_map/bd,drc->brc/dot_general | solution.py:27
  967.4 45.9 %copy.77 = bf16[256,192,300]{2,1,0:T(8,128)(2,1)} copy(bf16[256,192,300]{0,2,1:T(8,128)(2,1)} %convert_bitcast_fusion.1) | data formatting | bytes 58982400 | tf_op jit(solution)/shard_map/convert_element_type | solution.py:32
  1013.2 7.5 all-to-all-start.1
  1020.8 71.6 %fusion.8 = f32[300,300]{1,0:T(8,128)} fusion(bf16[32,1536,300]{1,0,2:T(8,128)(2,1)} %param.10, bf16[32,1536,300]{1,0,2:T(8,128)(2,1)} %broadcast_multiply_fusion), kind=kOutput, calls=%fused_computation.11 | convolution fusion | flops 8847360000 | bytes 59342400 | tf_op jit(solution)/shard_map/dot_general | solution.py:45
  1092.7 0.3 copy.80
  1093.0 16.5 all_gather.3
  1109.5 3.2 gather_fusion
  1112.7 0.3 convert_bitcast_fusion.2
  1113.0 0.2 copy.81
  1113.2 1.3 fusion.13
  1114.5 787.4 %all-reduce.2.cloned.1.call-done = f32[300,300]{1,0:T(8,128)} async-done(((f32[300,300]{1,0:T(8,128)}), f32[300,300]{1,0:T(8,128)}) %all-reduce.2.cloned.1.call-update) | async-done | bytes 360016 | tf_op jit(solution)/shard_map/psum | solution.py:58
  1901.9 1.8 broadcast_multiply_fusion.1
  1903.8 36.0 %convert_bitcast_fusion = f32[32,8,192,300]{3,2,0,1:T(8,128)} fusion(bf16[8,32,192,300]{3,2,1,0:T(8,128)(2,1)} %bitcast.12), kind=kLoop, calls=%fused_computation.1 | loop fusion | flops 14745600 | bytes 88473600 | tf_op jit(solution)/shard_map/convert_element_type | solution.py:51
  1939.8 90.5 %copy.90 = f32[32,8,192,300]{2,1,3,0:T(8,128)} copy(f32[32,8,192,300]{3,2,0,1:T(8,128)} %convert_bitcast_fusion) | data formatting | bytes 117964800 | tf_op jit(solution)/shard_map/convert_element_type | solution.py:51
  2030.3 64.1 %reshape.67 = f32[32,1536,300]{1,2,0:T(8,128)} reshape(f32[32,8,192,300]{2,1,3,0:T(8,128)} %copy.90) | data formatting | bytes 117964800 | tf_op jit(solution)/shard_map/convert_element_type | solution.py:51
  2094.5 48.1 %multiply_convert_fusion = bf16[32,1536,300]{1,2,0:T(8,128)(2,1)} fusion(f32[32,1536,300]{1,2,0:T(8,128)} %reshape.67, f32[32,1536]{1,0:T(8,128)S(1)} %bitcast.32, f32[1536,300]{0,1:T(8,128)S(1)} %fusion.13, f32[32,1536]{1,0:T(8,128)S(1)} %copy.81, bf16[32,1536,300]{1,0,2:T(8,128)(2,1)} %broadcast_multiply_fusion, bf16[300,300]{1,0:T(8,128)(2,1)S(1)} %copy-done), kind=kOutput, calls=%fused_computation.2 | convolution fusion | flops 8921088000 | bytes 120381216 | tf_op jit(solution)/shard_map/dot_general | solution.py:42
  2142.6 20.6 copy.85
  (24 shorter events, 0.4 us)
Async XLA Ops:
  7.2 2087.3 %copy-start = (bf16[300,300]{1,0:T(8,128)(2,1)S(1)}, bf16[300,300]{1,0:T(8,128)(2,1)}, u32[]{:S(2)}) copy-start(bf16[300,300]{1,0:T(8,128)(2,1)} %param.12) | copy-start | bytes 540004
  903.5 25.6 %copy-start.1 = (bf16[256,256]{1,0:T(8,128)(2,1)S(1)}, bf16[256,256]{1,0:T(8,128)(2,1)}, u32[]{:S(2)}) copy-start(bf16[256,256]{1,0:T(8,128)(2,1)} %param.13) | copy-start | bytes 393220
  1013.2 890.5 %all-to-all-start.1 = ((bf16[256,192,300]{2,1,0:T(8,128)(2,1)}), bf16[256,192,300]{2,1,0:T(8,128)(2,1)}, u32[]{:S(2)}, u32[]{:S(2)}) async-start(bf16[256,192,300]{2,1,0:T(8,128)(2,1)} %copy.77), calls=%async_computation.1 | async-start | bytes 75497472 | tf_op jit(solution)/shard_map/all_to_all | solution.py:33
  1020.7 71.7 %copy-start.5 = (f32[32,6]{0,1:T(8,128)S(1)}, f32[32,6]{0,1:T(8,128)}, u32[]{:S(2)}) copy-start(f32[32,6]{0,1:T(8,128)} %get-tuple-element.12) | copy-start | bytes 2308
  1020.7 72.0 %copy-start.2 = (bf16[32,2048]{1,0:T(8,128)(2,1)S(1)}, bf16[32,2048]{1,0:T(8,128)(2,1)}, u32[]{:S(2)}) copy-start(bf16[32,2048]{1,0:T(8,128)(2,1)} %param.14) | copy-start | bytes 393220
  1020.7 72.3 %copy-start.3 = (s32[1536]{0:T(1024)S(1)}, s32[1536]{0:T(1024)}, u32[]{:S(2)}) copy-start(s32[1536]{0:T(1024)} %param.16) | copy-start | bytes 18436
  1020.8 92.5 %copy-start.4 = (bf16[30,300]{1,0:T(8,128)(2,1)S(1)}, bf16[30,300]{1,0:T(8,128)(2,1)}, u32[]{:S(2)}) copy-start(bf16[30,300]{1,0:T(8,128)(2,1)} %param.15) | copy-start | bytes 54004
  1020.8 92.5 %copy-start.6 = (s32[1536]{0:T(1024)S(1)}, s32[1536]{0:T(1024)}, u32[]{:S(2)}) copy-start(s32[1536]{0:T(1024)} %param.17) | copy-start | bytes 18436
  1020.8 881.2 %all-reduce.2.cloned.1.call-start = ((), (), s32[]{:S(2)}) async-start(), calls=%async_computation.2 | async-start | bytes 933888 | tf_op jit(solution)/shard_map/psum | solution.py:58
Sparse Core Ops, SparseCore 0:
  1092.6 809.3 all-reduce.1
where the time goes:
time: 2180 us; the launch traced here: 2170 us
  blocking collectives  842 us (39%)
  waiting for transfers between devices  787 us (36%)
  local copies, waits for them, and re-layouts  300 us (14%)
  matrix products  159 us (7%)
  other arithmetic  59.7 us (3%)
    all_to_all x1, blocking collectives, body(): lax.all_to_all(masked, 'tile', split_axis=1, concat_axis=0, tiled=True)  826 us
    psum x1, waiting for transfers between devices, body(): density = lax.psum(partial_value, ('tile', 'grp')) / norm_scale  787 us
    convert_element_type x2, local copies, waits for them, and re-layouts, body(): summed = vv_term + slab_term.astype(jnp.float32) + pair_term  155 us
    dot_general x1, matrix products, body(): lax.dot_general(flat_rows, right_triples.reshape(-1, feature), (((0,), (0...  71.6 us
    mul x2, local copies, waits for them, and re-layouts, body(): left_triples.reshape(slab_count, tile_count, tile_rows, feature)  48.7 us
    dot_general x1, matrix products, body(): jnp.dot(flat_rows, vv_block, preferred_element_type=jnp.float32)  48.1 us
    convert_element_type x1, local copies, waits for them, and re-layouts, body(): mixed_rows = jnp.einsum('bd,drc->brc', slab_block, lax.all_to_all(masked,...  45.9 us
  transfers between devices with their start and end apart: 2, of which 1 were waited for; matrix products, arithmetic and copies ran while one was open for 4% of the time, Pallas kernels for 0%

commit v1 on v0

--- a/solution.py
+++ b/solution.py
@@ -27,7 +27,12 @@
     mixed_rows = jnp.einsum(
         "bd,drc->brc",
         slab_block,
-        lax.all_to_all(masked, "tile", split_axis=1, concat_axis=0, tiled=True),
+        jnp.concatenate(
+            lax.all_to_all(
+                jnp.stack(jnp.split(masked, lax.axis_size("tile"), axis=1)), "tile", 0, 0
+            ),
+            axis=0,
+        ),
         preferred_element_type=jnp.float32,
     ).astype(jnp.bfloat16)
     slab_term = lax.all_to_all(mixed_rows, "tile", split_axis=0, concat_axis=1, tiled=True)

time: 2180 us -> 2190 us (level)
  matrix products: 159 us -> 121 us
  waiting for transfers between devices: 787 us -> 822 us
    unnamed x18 -> x26, local copies, waits for them, and re-layouts: 21.1 us -> 99.8 us
    mul x2 -> x1, local copies, waits for them, and re-layouts: 48.7 us -> 0.1 us  [body(): left_triples.reshape(slab_count, tile_count, tile_rows, feature)]
    dot_general x1, matrix products: 71.6 us -> 37 us  [body(): lax.dot_general(flat_rows, right_triples.reshape(-1, feature), (((0,), (0...]
    psum x1, waiting for transfers between devices: 787 us -> 822 us  [body(): density = lax.psum(partial_value, ('tile', 'grp')) / norm_scale]
    all_to_all x1 -> x0, local copies, waits for them, and re-layouts: 25.6 us -> none  [body(): lax.all_to_all(masked, 'tile', split_axis=1, concat_axis=0, tiled=True)]
  transfers between devices with their start and end apart: 2 -> 2, of which waited for: 1 -> 1; matrix products, arithmetic and copies ran while one was open for 4% -> 2% of each run, Pallas kernels for 0% -> 0%
where the time goes in v1:
time: 2190 us; the launch traced here: 2180 us
  blocking collectives  843 us (38%)
  waiting for transfers between devices  822 us (38%)
  local copies, waits for them, and re-layouts  309 us (14%)
  matrix products  121 us (6%)
  other arithmetic  65.1 us (3%)
    all_to_all x1, blocking collectives, body(): lax.all_to_all(jnp.stack(jnp.split(masked, lax.axis_size('tile'), axis=1)...  826 us
    psum x1, waiting for transfers between devices, body(): density = lax.psum(partial_value, ('tile', 'grp')) / norm_scale  822 us
    convert_element_type x2, local copies, waits for them, and re-layouts, body(): summed = vv_term + slab_term.astype(jnp.float32) + pair_term  155 us
    unnamed x26, local copies, waits for them, and re-layouts  99.8 us
    convert_element_type x1, local copies, waits for them, and re-layouts, body(): mixed_rows = jnp.einsum('bd,drc->brc', slab_block, jnp.concatenate(lax.al...  45.9 us
    dot_general x1, matrix products, body(): jnp.dot(flat_rows, vv_block, preferred_element_type=jnp.float32)  44.2 us
  transfers between devices with their start and end apart: 2, of which 1 were waited for; matrix products, arithmetic and copies ran while one was open for 2% of the time, Pallas kernels for 0%

profile of v1, /device:TPU:0, one launch (start us, length us, event | category | flops | bytes accessed | tf_op | source)
XLA Modules:
  0.0 2181.4 jit_solution(8407940999646100742)
XLA Ops:
  8.8 44.0 %copy.37 = bf16[32,1536,300]{2,1,0:T(8,128)(2,1)} copy(bf16[32,1536,300]{1,0,2:T(8,128)(2,1)} %param.9) | data formatting | bytes 58982400 | tf_op args[0]
  52.7 25.6 %broadcast_multiply_fusion = bf16[32,1536,300]{2,1,0:T(8,128)(2,1)} fusion(bf16[32,1536,300]{2,1,0:T(8,128)(2,1)} %copy.37, bf16[32,1536]{1,0:T(8,128)(2,1)S(1)} %bitcast.64), kind=kLoop, calls=%fused_computation.8 | loop fusion | flops 14745600 | bytes 59080704 | tf_op jit(solution)/shard_map/mul | solution.py:24
  78.3 5.0 fusion.13
  83.3 5.0 fusion.12
  88.3 4.9 fusion.11
  93.2 4.9 fusion.10
  98.2 5.0 fusion.9
  103.1 5.0 fusion.8
  108.1 4.9 fusion.7
  113.1 4.9 fusion.6
  118.0 826.2 %all_to_all.14 = bf16[8,32,192,300]{3,2,1,0:T(8,128)(2,1)} all-to-all(bf16[8,32,192,300]{3,2,1,0:T(8,128)(2,1)} %fusion.6), channel_id=1, replica_groups=mesh['tile'=8,'grp'=4] {'tile'}, dimensions={0} | all-to-all | bytes 58982400 | tf_op jit(solution)/shard_map/all_to_all | solution.py:31
  944.2 38.2 %convert_bitcast_fusion.1 = bf16[256,192,300]{0,2,1:T(8,128)(2,1)} fusion(bf16[256,192,300]{2,1,0:T(8,128)(2,1)} %bitcast.60, bf16[256,256]{1,0:T(8,128)(2,1)S(1)} %copy-done.1), kind=kOutput, calls=%fused_computation.7 | convolution fusion | flops 7564492800 | bytes 59113472 | tf_op jit(solution)/shard_map/bd,drc->brc/dot_general | solution.py:27
  982.4 45.9 %copy.41 = bf16[256,192,300]{2,1,0:T(8,128)(2,1)} copy(bf16[256,192,300]{0,2,1:T(8,128)(2,1)} %convert_bitcast_fusion.1) | data formatting | bytes 58982400 | tf_op jit(solution)/shard_map/convert_element_type | solution.py:37
  1028.3 7.5 all-to-all-start.1
  1036.1 37.0 %fusion.14 = f32[300,300]{1,0:T(8,128)} fusion(bf16[32,1536,300]{2,1,0:T(8,128)(2,1)} %broadcast_multiply_fusion, bf16[32,1536,300]{1,0,2:T(8,128)(2,1)} %param.10), kind=kOutput, calls=%fused_computation.25 | convolution fusion | flops 8847360000 | bytes 59342400 | tf_op jit(solution)/shard_map/dot_general | solution.py:50
  1073.7 16.7 all_gather.3
  1090.4 3.2 gather_fusion
  1095.4 821.7 %all-reduce.2.cloned.1.call-done = f32[300,300]{1,0:T(8,128)} async-done(((f32[300,300]{1,0:T(8,128)}), f32[300,300]{1,0:T(8,128)}) %all-reduce.2.cloned.1.call-update) | async-done | bytes 360016 | tf_op jit(solution)/shard_map/psum | solution.py:63
  1917.1 1.8 broadcast_multiply_fusion.1
  1919.0 36.0 %convert_bitcast_fusion = f32[32,8,192,300]{3,2,0,1:T(8,128)} fusion(bf16[8,32,192,300]{3,2,1,0:T(8,128)(2,1)} %bitcast.16), kind=kLoop, calls=%fused_computation.1 | loop fusion | flops 14745600 | bytes 88473600 | tf_op jit(solution)/shard_map/convert_element_type | solution.py:56
  1955.0 90.5 %copy.54 = f32[32,8,192,300]{2,1,3,0:T(8,128)} copy(f32[32,8,192,300]{3,2,0,1:T(8,128)} %convert_bitcast_fusion) | data formatting | bytes 117964800 | tf_op jit(solution)/shard_map/convert_element_type | solution.py:56
  2045.5 64.1 %reshape.71 = f32[32,1536,300]{1,2,0:T(8,128)} reshape(f32[32,8,192,300]{2,1,3,0:T(8,128)} %copy.54) | data formatting | bytes 117964800 | tf_op jit(solution)/shard_map/convert_element_type | solution.py:56
  2109.7 44.2 %multiply_convert_fusion = bf16[32,1536,300]{1,2,0:T(8,128)(2,1)} fusion(f32[32,1536,300]{1,2,0:T(8,128)} %reshape.71, bf16[32,1536,300]{2,1,0:T(8,128)(2,1)} %broadcast_multiply_fusion, f32[32,1536]{1,0:T(8,128)S(1)} %bitcast.62, f32[1536,300]{0,1:T(8,128)S(1)} %fusion.17, f32[32,1536]{1,0:T(8,128)S(1)} %copy.45, bf16[300,300]{1,0:T(8,128)(2,1)S(1)} %copy-done), kind=kOutput, calls=%fused_computation.2 | convolution fusion | flops 8921088000 | bytes 120381216 | tf_op jit(solution)/shard_map/dot_general | solution.py:47
  2153.9 20.6 copy.49
  (31 shorter events, 4.2 us)
Async XLA Ops:
  7.2 2102.5 %copy-start = (bf16[300,300]{1,0:T(8,128)(2,1)S(1)}, bf16[300,300]{1,0:T(8,128)(2,1)}, u32[]{:S(2)}) copy-start(bf16[300,300]{1,0:T(8,128)(2,1)} %param.12) | copy-start | bytes 540004
  118.0 826.2 %copy-start.1 = (bf16[256,256]{1,0:T(8,128)(2,1)S(1)}, bf16[256,256]{1,0:T(8,128)(2,1)}, u32[]{:S(2)}) copy-start(bf16[256,256]{1,0:T(8,128)(2,1)} %param.13) | copy-start | bytes 393220
  1028.3 890.7 %all-to-all-start.1 = ((bf16[256,192,300]{2,1,0:T(8,128)(2,1)}), bf16[256,192,300]{2,1,0:T(8,128)(2,1)}, u32[]{:S(2)}, u32[]{:S(2)}) async-start(bf16[256,192,300]{2,1,0:T(8,128)(2,1)} %copy.41), calls=%async_computation.1 | async-start | bytes 75497472 | tf_op jit(solution)/shard_map/all_to_all | solution.py:38
  1035.7 37.4 %copy-start.5 = (f32[32,6]{0,1:T(8,128)S(1)}, f32[32,6]{0,1:T(8,128)}, u32[]{:S(2)}) copy-start(f32[32,6]{0,1:T(8,128)} %get-tuple-element.8) | copy-start | bytes 2308
  1035.8 37.6 %copy-start.2 = (bf16[32,2048]{1,0:T(8,128)(2,1)S(1)}, bf16[32,2048]{1,0:T(8,128)(2,1)}, u32[]{:S(2)}) copy-start(bf16[32,2048]{1,0:T(8,128)(2,1)} %param.14) | copy-start | bytes 393220
  1035.8 37.9 %copy-start.3 = (s32[1536]{0:T(1024)S(1)}, s32[1536]{0:T(1024)}, u32[]{:S(2)}) copy-start(s32[1536]{0:T(1024)} %param.16) | copy-start | bytes 18436
  1035.8 58.4 %copy-start.4 = (bf16[30,300]{1,0:T(8,128)(2,1)S(1)}, bf16[30,300]{1,0:T(8,128)(2,1)}, u32[]{:S(2)}) copy-start(bf16[30,300]{1,0:T(8,128)(2,1)} %param.15) | copy-start | bytes 54004
  1035.8 58.4 %copy-start.6 = (s32[1536]{0:T(1024)S(1)}, s32[1536]{0:T(1024)}, u32[]{:S(2)}) copy-start(s32[1536]{0:T(1024)} %param.17) | copy-start | bytes 18436
  1035.8 881.3 %all-reduce.2.cloned.1.call-start = ((), (), s32[]{:S(2)}) async-start(), calls=%async_computation.2 | async-start | bytes 933888 | tf_op jit(solution)/shard_map/psum | solution.py:63
Sparse Core Ops, SparseCore 0:
  1073.2 843.8 all-reduce.1
